TPU v7x, 128 devices: a whole 4x4x4 slice. The times are simulated.
128 devices in a mesh: grp: 2 (over y_lo), row: 16 (over x, z), hid: 4 (over y_hi, core).
Axes of the slice: x: 4, y: 4 (y_hi: 2, y_lo: 2; y = y_hi * 2 + y_lo), z: 4, core: 2. Of those that a mesh axis runs over, the one named last changes fastest.
Arguments:
- token_ids: int32 [512, 64], P(('grp', 'row')), may hold values from 0 to 128255, as said below
- activations: bfloat16 [512, 64, 4096], P(('grp', 'row'), None, 'hid'), may hold values from -6 to 6
- out_grads: bfloat16 [512, 64, 4096], P(('grp', 'row'), None, 'hid'), may hold values from -6 to 6
- proj_in: bfloat16 [64, 4096], P(None, 'hid'), may hold values from -0.09375 to 0.09375
- proj_out: bfloat16 [64, 4096], P(None, 'hid'), may hold values from -0.09375 to 0.09375
- inverse_curvature: float32 [4096, 4096], P('row', ('grp', 'hid')), as said below
- store_grads: bfloat16 [262144, 4096], P(('grp', 'row', 'hid')), may hold values from -1 to 1
- store_order: int32 [262144], P(('grp', 'row', 'hid')), may hold values from 0 to 262143, each once
- example_ids: int32 [512], replicated, may hold values from 0 to 262143
Outputs:
- scores: bfloat16 [262144, 512], P(('grp', 'row', 'hid'))
Inputs may be any that keep to these rules, and one draw needn't show every extreme that they name: `token_ids`: 0 marks padding, which only follows a query's tokens; each query has at least 16 tokens that are not padding. `example_ids`: each query's id names a stored example. `inverse_curvature`: symmetric.
All inputs are finite; a program needn't handle non-finite values.
Results may differ from a plain program's by a relative error of at most 0.013.
Values may be sent and summed in bfloat16 or wider, within the bound.
No kernel may reach another device: no remote copies, remote signals or barrier semaphores. Data moves between devices by JAX's collectives and lax.ppermute only.
A program may use at most 128 MiB of HBM per device.

v0:
```python
import functools

import jax
import jax.numpy as jnp
from jax import lax
from jax.experimental import pallas as pl
from jax.experimental.pallas import tpu as pltpu
from jax.sharding import PartitionSpec as P


AXES = ("grp", "row", "hid")
NT = (((1,), (1,)), ((), ()))
TN = (((0,), (0,)), ((), ()))
F32 = jnp.float32
BF16 = jnp.bfloat16
VMEM = pl.BlockSpec(memory_space=pltpu.VMEM)
HBM = pl.BlockSpec(memory_space=pltpu.HBM)
TILE = 512
STEPS = (1, 3, 2)


def linear(x, y, z, core):
    return (y % 2) * 64 + (x * 4 + z) * 4 + (y // 2) * 2 + core


def everywhere():
    return [(x, y, z, core) for x in range(4) for y in range(4) for z in range(4) for core in range(2)]


def moved(value, target):
    pairs = [(linear(*place), linear(*target(*place))) for place in everywhere()]
    return lax.ppermute(value, AXES, pairs)


def across(value):
    return moved(value, lambda x, y, z, core: (x, y, z, 1 - core))


def along_y(value, step):
    return moved(value, lambda x, y, z, core: (x, (y + step) % 4, z, core))


def along_line(value, step):
    return moved(
        value,
        lambda x, y, z, core: (x, y, (z + step) % 4, 1) if core else ((x + step) % 4, y, z, 0),
    )


def copied(value, key):
    found = {}
    for place in sorted(everywhere(), key=lambda place: linear(*place)):
        found.setdefault(key(*place), []).append(linear(*place))
    groups = list(found.values())
    count = len(groups[0])
    return lax.all_to_all(
        jnp.broadcast_to(value[None], (count, *value.shape)), AXES, 0, 0, axis_index_groups=groups, tiled=True
    )


def in_hbm(value):
    return pltpu.with_memory_space_constraint(value, pltpu.HBM)


def core_and_half():
    hid = lax.axis_index("hid")
    return hid & 1, hid >> 1


def packed(inside, outside):
    return (
        jnp.concatenate([inside[:256], inside[256:]], axis=1),
        jnp.concatenate([outside[128 * i : 128 * (i + 1)] for i in range(4)], axis=1),
    )


def project_kernel(grads, inputs, w_out, w_in, send, keep, grads_in, inputs_in, out_sorted, in_held, sem, w_sem):
    core, half = core_and_half()
    weights, tiles = [pltpu.make_async_copy(w_in, in_held, w_sem.at[8])], []
    for side in range(2):
        for part in range(4):
            rows = pl.ds(pl.multiple_of((2 * part + (core ^ side)) * 8, 8), 8)
            weights.append(
                pltpu.make_async_copy(
                    w_out.at[rows, :], out_sorted.at[pl.ds(side * 32 + part * 8, 8), :], w_sem.at[side * 4 + part]
                )
            )
    for i in range(4):
        start = (1 - half if i < 2 else half) * 512 + i % 2 * 256
        rows = pl.ds(pl.multiple_of(start, 256), 256)
        tiles.append(pltpu.make_async_copy(inputs.at[rows, :], inputs_in.at[i], sem.at[2 * i]))
        tiles.append(pltpu.make_async_copy(grads.at[rows, :], grads_in.at[i], sem.at[2 * i + 1]))
    for copy in weights + tiles:
        copy.start()
    for copy in weights:
        copy.wait()
    for n in range(2):
        outside, inside = [], []
        for i in (2 * n, 2 * n + 1):
            tiles[2 * i].wait()
            inside.append(lax.dot_general(inputs_in[i], in_held[...], NT, preferred_element_type=F32))
            tiles[2 * i + 1].wait()
            outside.append(lax.dot_general(grads_in[i], out_sorted[...], NT, preferred_element_type=F32))
        outside, inside = jnp.concatenate(outside, axis=0), jnp.concatenate(inside, axis=0)
        ends = ((384 * n, 384 * n + 256), (384 * n + 256, 384 * n + 384))
        for (first, last), value in zip(ends, packed(inside, outside[:, :32])):
            keep[first:last] = value
        for (first, last), value in zip(ends, packed(inside, outside[:, 32:])):
            send[first:last] = value.astype(BF16)


def project(grads, inputs, w_out, w_in):
    tokens, width = grads.shape
    return pl.pallas_call(
        project_kernel,
        out_shape=(jax.ShapeDtypeStruct((768, 128), BF16), jax.ShapeDtypeStruct((768, 128), F32)),
        in_specs=[HBM] * 4,
        out_specs=(VMEM, VMEM),
        scratch_shapes=[
            pltpu.VMEM((4, 256, width), BF16),
            pltpu.VMEM((4, 256, width), BF16),
            pltpu.VMEM((64, width), BF16),
            pltpu.VMEM((64, width), BF16),
            pltpu.SemaphoreType.DMA((8,)),
            pltpu.SemaphoreType.DMA((9,)),
        ],
        cost_estimate=pl.CostEstimate(
            flops=2 * tokens * width * 128, bytes_accessed=2 * tokens * width * 2, transcendentals=0
        ),
        compiler_params=pltpu.CompilerParams(vmem_limit_bytes=12 << 20),
        name="project",
    )(in_hbm(grads), in_hbm(inputs), in_hbm(w_out), in_hbm(w_in))


def outer_kernel(ids, keep, came, came_half, out, held):
    _, half = core_and_half()
    usable = (ids[pl.ds(pl.multiple_of(half * 8, 8), 8), :] > 0).astype(F32)
    counts = jnp.sum(usable, axis=1, keepdims=True)
    total = keep[384:] + came[384:].astype(F32) + came_half[...].astype(F32)
    position = lax.broadcasted_iota(jnp.int32, (64, 32), 0).astype(F32)
    for q in range(8):
        count = counts[q : q + 1]
        inside = total[64 * (q % 4) : 64 * (q % 4 + 1), 64 * (q // 4) : 64 * (q // 4 + 1)]
        outside = total[256 + 64 * (q % 2) : 320 + 64 * (q % 2), 32 * (q // 2) : 32 * (q // 2 + 1)]
        outside = jnp.where(position < count, outside, 0.0)
        held[q] = (
            lax.dot_general(outside.astype(BF16), inside.astype(BF16), TN, preferred_element_type=F32) / count
        )
        even, odd = held[q, pl.ds(0, 16, 2), :], held[q, pl.ds(1, 16, 2), :]
        out[q] = jnp.concatenate([even, odd], axis=1).astype(BF16)


def outer(ids, keep, came, came_half):
    return pl.pallas_call(
        outer_kernel,
        out_shape=jax.ShapeDtypeStruct((8, 16, 128), BF16),
        in_specs=[VMEM] * 4,
        out_specs=VMEM,
        scratch_shapes=[pltpu.VMEM((8, 32, 64), F32)],
        compiler_params=pltpu.CompilerParams(vmem_limit_bytes=8 << 20),
        name="outer",
    )(ids, keep, came, came_half)


def precondition_kernel(grads, own, behind, ahead, across_ring, keep, send):
    core, half = core_and_half()
    y = half * 2 + lax.axis_index("grp")
    total = jnp.zeros((128, 256), F32)
    for block, step in ((own, 0), (behind, 1), (ahead, 3), (across_ring, 2)):
        there = (y - step) & 3
        start = pl.multiple_of(((there & 1) * 2 + (there >> 1)) * 512, 512)
        total += lax.dot_general(grads[:, pl.ds(start, 512)], block[...], NT, preferred_element_type=F32)
    low, high = total[:, :128], total[:, 128:]

    @pl.when(core == 0)
    def _():
        keep[...], send[...] = low, high.astype(BF16)

    @pl.when(core != 0)
    def _():
        keep[...], send[...] = high, low.astype(BF16)


def precondition(grads, blocks):
    return pl.pallas_call(
        precondition_kernel,
        out_shape=(jax.ShapeDtypeStruct((128, 128), F32), jax.ShapeDtypeStruct((128, 128), BF16)),
        in_specs=[VMEM] * 5,
        out_specs=(VMEM, VMEM),
        compiler_params=pltpu.CompilerParams(vmem_limit_bytes=8 << 20),
        name="precondition",
    )(grads, *blocks)


def partial_product(sources, store, blocks, i):
    rows = pl.ds(pl.multiple_of(i * TILE, TILE), TILE)
    core, _ = core_and_half()
    row = lax.axis_index("row")
    total = None
    for (other, step), block in zip(sources, blocks):
        owner = core ^ other
        line = (jnp.where(owner == 0, row >> 2, row & 3) - step) & 3
        stored = []
        for plane in range(4):
            column = jnp.where(owner == 0, 8 * line + 2 * plane, 8 * plane + 2 * line + 1)
            stored.append(store[rows, pl.ds(pl.multiple_of(column * 128, 128), 128)])
        term = lax.dot_general(
            jnp.concatenate(stored, axis=1),
            jnp.concatenate([block[plane] for plane in range(4)], axis=1),
            NT,
            preferred_element_type=F32,
        )
        total = term if total is None else total + term
    return rows, total


def first_kernel(store, own, out, held, sem):
    depth = store.shape[0]
    copies = [
        pltpu.make_async_copy(store.at[pl.ds(i, TILE), :], held.at[pl.ds(i, TILE), :], sem.at[i // TILE])
        for i in range(0, depth, TILE)
    ]
    for copy in copies:
        copy.start()
    for i, copy in enumerate(copies):
        copy.wait()
        out[i * TILE : (i + 1) * TILE, :] = partial_product([(0, 0)], held, [own], i)[1]


def first(store, own):
    depth = store.shape[0]
    return pl.pallas_call(
        first_kernel,
        out_shape=(pltpu.VMEM((depth, 512), F32), pltpu.VMEM(store.shape, store.dtype)),
        in_specs=[HBM, VMEM],
        out_specs=(VMEM, VMEM),
        scratch_shapes=[pltpu.SemaphoreType.DMA((depth // TILE,))],
        cost_estimate=pl.CostEstimate(
            flops=2 * depth * 512 * 512, bytes_accessed=2 * store.size * 2, transcendentals=0
        ),
        compiler_params=pltpu.CompilerParams(vmem_limit_bytes=12 << 20),
        name="first",
    )(in_hbm(store), own)


def next_kernel(sources, store, *refs):
    *blocks, before, out = refs

    @pl.loop(0, store.shape[0] // TILE)
    def _(i):
        rows, total = partial_product(sources, store, blocks, i)
        out[rows, :] = before[rows, :] + total


def last_kernel(sources, store, *refs):
    *blocks, before, order, ids, out, ready, sem = refs

    def leave(i):
        rows = pl.ds(pl.multiple_of(i * TILE, TILE), TILE)
        return pltpu.make_async_copy(ready.at[rows, :], out.at[rows, :], sem.at[i])

    @pl.loop(0, store.shape[0] // TILE)
    def _(i):
        rows, total = partial_product(sources, store, blocks, i)
        total = total + before[rows, :]
        for n in range(TILE // 128):
            column = jnp.broadcast_to(order[pl.ds(i * (TILE // 128) + n, 1), :], (128, 128)).T
            for m in range(4):
                lanes = slice(128 * m, 128 * (m + 1))
                ready[pl.ds(pl.multiple_of(i * TILE + 128 * n, 128), 128), lanes] = jnp.where(
                    column == ids[:, lanes], 0.0, total[128 * n : 128 * (n + 1), lanes]
                ).astype(BF16)
        leave(i).start()

    @pl.loop(0, store.shape[0] // TILE)
    def _(i):
        leave(i).wait()


def product(kernel, sources, store, blocks, extra, out_shape, out_spec, scratch):
    depth = store.shape[0]
    return pl.pallas_call(
        functools.partial(kernel, sources),
        out_shape=out_shape,
        in_specs=[VMEM] * (1 + len(blocks) + len(extra)),
        out_specs=out_spec,
        scratch_shapes=scratch,
        cost_estimate=pl.CostEstimate(
            flops=2 * depth * 512 * 512 * len(blocks), bytes_accessed=depth * 512 * 4, transcendentals=0
        ),
        compiler_params=pltpu.CompilerParams(vmem_limit_bytes=12 << 20),
    )(store, *blocks, *extra)


def local(
    token_ids,
    activations,
    out_grads,
    proj_in,
    proj_out,
    inverse_curvature,
    store_grads,
    store_order,
    example_ids,
):
    width = activations.shape[2]
    flat_inputs = activations.reshape(-1, width)
    flat_grads = out_grads.reshape(-1, width)
    send, keep = project(flat_grads, flat_inputs, proj_out, proj_in)
    came = across(send)
    passed = (keep[:384] + came[:384].astype(F32)).astype(BF16)
    came_half = along_y(passed, 2)
    curvature = inverse_curvature.astype(BF16)
    blocks = [curvature] + [along_y(curvature, step) for step in STEPS]
    grads = outer(token_ids, keep, came, came_half)
    grads = lax.all_to_all(jnp.broadcast_to(grads[None], (16, 8, 16, 128)), "row", 0, 0, tiled=True)
    keep, send = precondition(grads.reshape(128, 2048), blocks)
    mine = (keep + across(send).astype(F32)).astype(BF16)
    own = copied(mine.reshape(16, 8, 128), lambda x, y, z, core: (core, z if core else x))
    own = own.reshape(2, 4, 2, 16, 8, 128).transpose(1, 0, 3, 2, 4, 5).reshape(4, 512, 128)
    near = {}
    for step in STEPS:
        near[step] = along_line(own, step)
    own_far = across(own)
    part, store = first(store_grads, own)
    depth = store.shape[0]

    def added(kernel, sources, blocks, before):
        out = pltpu.VMEM((depth, 512), F32)
        return product(kernel, sources, store, blocks, before, out, VMEM, [])

    near[1], near[3], part = lax.optimization_barrier((near[1], near[3], part))
    far = dict((step, across(near[step])) for step in (1, 3))
    part = added(next_kernel, [(1, 0), (0, 1), (0, 3)], [own_far, near[1], near[3]], [part])
    part = added(next_kernel, [(1, 1), (1, 3)], [far[1], far[3]], [part])
    near[2], part = lax.optimization_barrier((near[2], part))
    far[2] = across(near[2])
    part = added(next_kernel, [(0, 2)], [near[2]], [part])
    return product(
        last_kernel,
        [(1, 2)],
        store,
        [far[2]],
        [part, store_order.reshape(depth // 128, 128), example_ids[None, :]],
        jax.ShapeDtypeStruct((depth, 512), BF16),
        HBM,
        [pltpu.VMEM((depth, 512), BF16), pltpu.SemaphoreType.DMA((depth // TILE,))],
    )


def solution(mesh):
    placed = (
        P(("grp", "row"), None),
        P(("grp", "row"), None, "hid"),
        P(("grp", "row"), None, "hid"),
        P(None, "hid"),
        P(None, "hid"),
        P("row", ("grp", "hid")),
        P(("grp", "row", "hid"), None),
        P(("grp", "row", "hid")),
        P(),
    )

    return jax.shard_map(local, mesh=mesh, in_specs=placed, out_specs=P(("grp", "row", "hid"), None), check_vma=False)
```

profile of v0, /device:TPU:1, one launch (start us, length us, event | category | flops | bytes accessed | tf_op | source)
XLA Modules:
  0.0 88.2 jit_solution(14030897764497641840)
XLA Ops:
  0.0 5.5 %project.1 = (bf16[768,128]{1,0:T(8,128)(2,1)S(1)}, f32[768,128]{1,0:T(8,128)S(1)}) custom-call(bf16[1024,1024]{1,0:T(8,128)(2,1)} %bitcast.19, bf16[1024,1024]{1,0:T(8,128)(2,1)} %bitcast.20, bf16[64,1024]{1,0:T(8,128)(2,1)} %w_out.1, bf16[64,1024]{1,0:T(8,128)(2,1)} %w_in.1), custom_call_target="tpu_custom_call" | custom-call | flops 268435456 | bytes 4194304 | tf_op jit(solution)/shard_map/project/pallas_call | solution.py:114
  5.5 1.5 %collective-permute-start = (bf16[768,128]{1,0:T(8,128)(2,1)S(1)}, bf16[768,128]{1,0:T(8,128)(2,1)S(1)}, u32[]{:S(2)}, u32[]{:S(2)}) collective-permute-start(bf16[768,128]{1,0:T(8,128)(2,1)S(1)} %get-tuple-element.17), channel_id=1, source_target_pairs={{0,1},{1,0},{4,5},{5,4},{8,9},{9,8},{12,13},{13,12},{64,65},{65,64... | collective-permute-start | bytes 589832 | tf_op jit(solution)/shard_map/ppermute | solution.py:32
  7.0 1.1 %collective-permute-done.came = bf16[768,128]{1,0:T(8,128)(2,1)S(1)} collective-permute-done((bf16[768,128]{1,0:T(8,128)(2,1)S(1)}, bf16[768,128]{1,0:T(8,128)(2,1)S(1)}, u32[]{:S(2)}, u32[]{:S(2)}) %collective-permute-start) | collective-permute-done | bytes 196640 | tf_op jit(solution)/shard_map/ppermute | solution.py:32
  8.1 3.1 %collective-permute-start.1 = (bf16[384,128]{1,0:T(8,128)(2,1)S(1)}, bf16[384,128]{1,0:T(8,128)(2,1)S(1)}, u32[]{:S(2)}, u32[]{:S(2)}) collective-permute-start(bf16[384,128]{1,0:T(8,128)(2,1)S(1)} %add_convert_fusion), channel_id=1, source_target_pairs={{0,2},{1,3},{4,6},{5,7},{8,10},{9,11},{12,14},{13,15},{64,66},{65,... | collective-permute-start | bytes 294920 | tf_op jit(solution)/shard_map/ppermute | solution.py:32
  11.2 2.6 %collective-permute-done.1.came_half = bf16[384,128]{1,0:T(8,128)(2,1)S(1)} collective-permute-done((bf16[384,128]{1,0:T(8,128)(2,1)S(1)}, bf16[384,128]{1,0:T(8,128)(2,1)S(1)}, u32[]{:S(2)}, u32[]{:S(2)}) %collective-permute-start.1) | collective-permute-done | bytes 98336 | tf_op jit(solution)/shard_map/ppermute | solution.py:32
  14.3 0.9 %broadcast_in_dim.16 = bf16[16,8,16,128]{3,1,2,0:T(8,128)(2,1)} broadcast(bf16[8,16,128]{2,0,1:T(8,128)(2,1)S(1)} %copy.11), dimensions={1,2,3} | broadcast | bytes 557056 | tf_op jit(solution)/shard_map/broadcast_in_dim | solution.py:316
  15.2 7.6 %all-to-all-start = ((bf16[16,8,16,128]{3,1,2,0:T(8,128)(2,1)}), bf16[16,8,16,128]{3,1,2,0:T(8,128)(2,1)S(1)}, u32[]{:S(2)}, u32[]{:S(2)}) async-start(bf16[16,8,16,128]{3,1,2,0:T(8,128)(2,1)} %broadcast_in_dim.16), calls=%async_computation | async-start | bytes 1048576 | tf_op jit(solution)/shard_map/all_to_all | solution.py:316
  22.8 3.0 %collective-permute-start.4 = (bf16[256,512]{1,0:T(8,128)(2,1)S(1)}, bf16[256,512]{1,0:T(8,128)(2,1)S(1)}, u32[]{:S(2)}, u32[]{:S(2)}) collective-permute-start(bf16[256,512]{1,0:T(8,128)(2,1)S(1)} %convert_element_type.17.own), channel_id=1, source_target_pairs={{0,2},{1,3},{4,6},{5,7},{8,10},{9,11},{12,14},{13,15},{64,66},{65,... | collective-permute-start | bytes 786440 | tf_op jit(solution)/shard_map/ppermute | solution.py:32
  27.3 3.5 %collective-permute-done.4.across_ring = bf16[256,512]{1,0:T(8,128)(2,1)S(1)} collective-permute-done((bf16[256,512]{1,0:T(8,128)(2,1)S(1)}, bf16[256,512]{1,0:T(8,128)(2,1)S(1)}, u32[]{:S(2)}, u32[]{:S(2)}) %collective-permute-start.4) | collective-permute-done | bytes 262176 | tf_op jit(solution)/shard_map/ppermute | solution.py:32
  30.7 6.8 %collective-permute-done.3.ahead = bf16[256,512]{1,0:T(8,128)(2,1)S(1)} collective-permute-done((bf16[256,512]{1,0:T(8,128)(2,1)S(1)}, bf16[256,512]{1,0:T(8,128)(2,1)S(1)}, u32[]{:S(2)}, u32[]{:S(2)}) %collective-permute-start.3) | collective-permute-done | bytes 262176 | tf_op jit(solution)/shard_map/ppermute | solution.py:32
  38.0 1.6 %collective-permute-start.5 = (bf16[128,128]{1,0:T(8,128)(2,1)S(1)}, bf16[128,128]{1,0:T(8,128)(2,1)S(1)}, u32[]{:S(2)}, u32[]{:S(2)}) collective-permute-start(bf16[128,128]{1,0:T(8,128)(2,1)S(1)} %get-tuple-element.19), channel_id=1, source_target_pairs={{0,1},{1,0},{4,5},{5,4},{8,9},{9,8},{12,13},{13,12},{64,65},{65,64... | collective-permute-start | bytes 98312 | tf_op jit(solution)/shard_map/ppermute | solution.py:32
  39.7 0.9 collective-permute-done.5
  40.7 15.3 %all_to_all.10 = bf16[16,16,8,128]{3,2,1,0:T(8,128)(2,1)S(1)} all-to-all(bf16[16,16,8,128]{3,2,1,0:T(8,128)(2,1)S(1)} %broadcast_in_dim.18), channel_id=1, replica_groups={{0,2,4,6,8,10,12,14,64,66,68,70,72,74,76,78},{1,3,17,19,33,35,49,51,65,..., dimensions={0} | all-to-all | bytes 1048576 | tf_op jit(solution)/shard_map/all_to_all | solution.py:56
  56.0 2.6 %collective-permute-start.8 = (bf16[4,512,128]{2,1,0:T(8,128)(2,1)S(1)}, bf16[4,512,128]{2,1,0:T(8,128)(2,1)S(1)}, u32[]{:S(2)}, u32[]{:S(2)}) collective-permute-start(bf16[4,512,128]{2,1,0:T(8,128)(2,1)S(1)} %bitcast.11), channel_id=1, source_target_pairs={{0,48},{1,13},{4,52},{5,1},{8,56},{9,5},{12,60},{13,9},{64,112},{6... | collective-permute-start | bytes 1572872 | tf_op jit(solution)/shard_map/ppermute | solution.py:32
  58.6 3.2 %collective-permute-start.11 = (bf16[4,512,128]{2,1,0:T(8,128)(2,1)S(1)}, bf16[4,512,128]{2,1,0:T(8,128)(2,1)S(1)}, u32[]{:S(2)}, u32[]{:S(2)}) collective-permute-start(bf16[4,512,128]{2,1,0:T(8,128)(2,1)S(1)} %bitcast.13), channel_id=1, source_target_pairs={{0,1},{1,0},{4,5},{5,4},{8,9},{9,8},{12,13},{13,12},{64,65},{65,64... | collective-permute-start | bytes 1572872 | tf_op jit(solution)/shard_map/ppermute | solution.py:32
  61.8 6.4 %first.1 = (f32[2048,512]{1,0:T(8,128)S(1)}, bf16[2048,4096]{1,0:T(8,128)(2,1)S(1)}) custom-call(bf16[2048,4096]{1,0:T(8,128)(2,1)} %store.1, bf16[4,512,128]{2,1,0:T(8,128)(2,1)S(1)} %bitcast.14), custom_call_target="tpu_custom_call" | custom-call | flops 1073741824 | bytes 33554432 | tf_op jit(solution)/shard_map/first/pallas_call | solution.py:232
  68.2 4.0 %collective-permute-start.9 = (bf16[4,512,128]{2,1,0:T(8,128)(2,1)S(1)}, bf16[4,512,128]{2,1,0:T(8,128)(2,1)S(1)}, u32[]{:S(2)}, u32[]{:S(2)}) collective-permute-start(bf16[4,512,128]{2,1,0:T(8,128)(2,1)S(1)} %collective-permute-done.7.refs_1_), channel_id=1, source_target_pairs={{0,1},{1,0},{4,5},{5,4},{8,9},{9,8},{12,13},{13,12},{64,65},{65,64... | collective-permute-start | bytes 1572872 | tf_op jit(solution)/shard_map/ppermute | solution.py:32
  72.2 1.6 %collective-permute-start.6 = (bf16[4,512,128]{2,1,0:T(8,128)(2,1)S(1)}, bf16[4,512,128]{2,1,0:T(8,128)(2,1)S(1)}, u32[]{:S(2)}, u32[]{:S(2)}) collective-permute-start(bf16[4,512,128]{2,1,0:T(8,128)(2,1)S(1)} %bitcast.15), channel_id=1, source_target_pairs={{0,32},{1,9},{4,36},{5,13},{8,40},{9,1},{12,44},{13,5},{64,96},{65... | collective-permute-start | bytes 1572872 | tf_op jit(solution)/shard_map/ppermute | solution.py:32
  73.8 4.1 %shard_map.91.refs_2_ = f32[2048,512]{1,0:T(8,128)S(1)} custom-call(bf16[2048,4096]{1,0:T(8,128)(2,1)S(1)} %get-tuple-element.20.store, bf16[4,512,128]{2,1,0:T(8,128)(2,1)S(1)} %collective-permute-done.11.refs_0_, bf16[4,512,128]{2,1,0:T(8,128)(2,1)S(1)} %collective-permute-done.7.refs_1_, bf16[4,512,128]{2,1,0:T(8,128)(2,1)S(1)} %collective-permute-done.8.refs_2_, ...), custom_call_target="tpu_custom_call" | custom-call | flops 3221225472 | bytes 4194304 | tf_op jit(solution)/shard_map/pallas_call | solution.py:282
  78.0 3.0 %shard_map.92.refs_1_ = f32[2048,512]{1,0:T(8,128)S(1)} custom-call(bf16[2048,4096]{1,0:T(8,128)(2,1)S(1)} %get-tuple-element.20.store, bf16[4,512,128]{2,1,0:T(8,128)(2,1)S(1)} %collective-permute-done.9.refs_0_, bf16[4,512,128]{2,1,0:T(8,128)(2,1)S(1)} %collective-permute-done.10.refs_1_, f32[2048,512]{1,0:T(8,128)S(1)} %shard_map.91.refs_2_), custom_call_target="tpu_custom_call" | custom-call | flops 2147483648 | bytes 4194304 | tf_op jit(solution)/shard_map/pallas_call | solution.py:282
  81.0 1.0 %collective-permute-done.6.refs_0_ = bf16[4,512,128]{2,1,0:T(8,128)(2,1)S(1)} collective-permute-done((bf16[4,512,128]{2,1,0:T(8,128)(2,1)S(1)}, bf16[4,512,128]{2,1,0:T(8,128)(2,1)S(1)}, u32[]{:S(2)}, u32[]{:S(2)}) %collective-permute-start.6) | collective-permute-done | bytes 524320 | tf_op jit(solution)/shard_map/ppermute | solution.py:32
  82.1 1.4 %collective-permute-start.12 = (bf16[4,512,128]{2,1,0:T(8,128)(2,1)S(1)}, bf16[4,512,128]{2,1,0:T(8,128)(2,1)S(1)}, u32[]{:S(2)}, u32[]{:S(2)}) collective-permute-start(bf16[4,512,128]{2,1,0:T(8,128)(2,1)S(1)} %collective-permute-done.6.refs_0_), channel_id=1, source_target_pairs={{0,1},{1,0},{4,5},{5,4},{8,9},{9,8},{12,13},{13,12},{64,65},{65,64... | collective-permute-start | bytes 1572872 | tf_op jit(solution)/shard_map/ppermute | solution.py:32
  83.4 1.9 %shard_map.93.refs_1_ = f32[2048,512]{1,0:T(8,128)S(1)} custom-call(bf16[2048,4096]{1,0:T(8,128)(2,1)S(1)} %get-tuple-element.20.store, bf16[4,512,128]{2,1,0:T(8,128)(2,1)S(1)} %collective-permute-done.6.refs_0_, f32[2048,512]{1,0:T(8,128)S(1)} %shard_map.92.refs_1_), custom_call_target="tpu_custom_call" | custom-call | flops 1073741824 | bytes 4194304 | tf_op jit(solution)/shard_map/pallas_call | solution.py:282
  85.4 2.8 %shard_map.94 = bf16[2048,512]{1,0:T(8,128)(2,1)} custom-call(bf16[2048,4096]{1,0:T(8,128)(2,1)S(1)} %get-tuple-element.20.store, bf16[4,512,128]{2,1,0:T(8,128)(2,1)S(1)} %collective-permute-done.12.refs_0_, f32[2048,512]{1,0:T(8,128)S(1)} %shard_map.93.refs_1_, s32[16,128]{1,0:T(8,128)S(1)} %bitcast.17, s32[1,512]{1,0:T(1,128)S(1)} %bitcast.18), custom_call_target="tpu_custom_call" | custom-call | flops 1073741824 | bytes 4194304 | tf_op jit(solution)/shard_map/pallas_call | solution.py:282
  (28 shorter events, 2.7 us)
Async XLA Ops:
  0.0 13.8 %copy-start = (s32[16,64]{1,0:T(8,128)S(1)}, s32[16,64]{1,0:T(8,128)}, u32[]{:S(2)}) copy-start(s32[16,64]{1,0:T(8,128)} %ids.1) | copy-start | bytes 12292
  0.0 22.7 %copy-start.3 = (f32[256,512]{1,0:T(8,128)S(1)}, f32[256,512]{1,0:T(8,128)}, u32[]{:S(2)}) copy-start(f32[256,512]{1,0:T(8,128)} %param.14) | copy-start | bytes 1572868
  5.5 2.5 %collective-permute-start = (bf16[768,128]{1,0:T(8,128)(2,1)S(1)}, bf16[768,128]{1,0:T(8,128)(2,1)S(1)}, u32[]{:S(2)}, u32[]{:S(2)}) collective-permute-start(bf16[768,128]{1,0:T(8,128)(2,1)S(1)} %get-tuple-element.17), channel_id=1, source_target_pairs={{0,1},{1,0},{4,5},{5,4},{8,9},{9,8},{12,13},{13,12},{64,65},{65,64... | collective-permute-start | bytes 589832 | tf_op jit(solution)/shard_map/ppermute | solution.py:32
  8.1 5.7 %collective-permute-start.1 = (bf16[384,128]{1,0:T(8,128)(2,1)S(1)}, bf16[384,128]{1,0:T(8,128)(2,1)S(1)}, u32[]{:S(2)}, u32[]{:S(2)}) collective-permute-start(bf16[384,128]{1,0:T(8,128)(2,1)S(1)} %add_convert_fusion), channel_id=1, source_target_pairs={{0,2},{1,3},{4,6},{5,7},{8,10},{9,11},{12,14},{13,15},{64,66},{65,... | collective-permute-start | bytes 294920 | tf_op jit(solution)/shard_map/ppermute | solution.py:32
  15.2 22.4 %all-to-all-start = ((bf16[16,8,16,128]{3,1,2,0:T(8,128)(2,1)}), bf16[16,8,16,128]{3,1,2,0:T(8,128)(2,1)S(1)}, u32[]{:S(2)}, u32[]{:S(2)}) async-start(bf16[16,8,16,128]{3,1,2,0:T(8,128)(2,1)} %broadcast_in_dim.16), calls=%async_computation | async-start | bytes 1048576 | tf_op jit(solution)/shard_map/all_to_all | solution.py:316
  22.8 7.9 %collective-permute-start.4 = (bf16[256,512]{1,0:T(8,128)(2,1)S(1)}, bf16[256,512]{1,0:T(8,128)(2,1)S(1)}, u32[]{:S(2)}, u32[]{:S(2)}) collective-permute-start(bf16[256,512]{1,0:T(8,128)(2,1)S(1)} %convert_element_type.17.own), channel_id=1, source_target_pairs={{0,2},{1,3},{4,6},{5,7},{8,10},{9,11},{12,14},{13,15},{64,66},{65,... | collective-permute-start | bytes 786440 | tf_op jit(solution)/shard_map/ppermute | solution.py:32
  25.8 11.8 %collective-permute-start.3 = (bf16[256,512]{1,0:T(8,128)(2,1)S(1)}, bf16[256,512]{1,0:T(8,128)(2,1)S(1)}, u32[]{:S(2)}, u32[]{:S(2)}) collective-permute-start(bf16[256,512]{1,0:T(8,128)(2,1)S(1)} %convert_element_type.17.own), channel_id=1, source_target_pairs={{0,66},{1,67},{4,70},{5,71},{8,74},{9,75},{12,78},{13,79},{64,0},{... | collective-permute-start | bytes 786440 | tf_op jit(solution)/shard_map/ppermute | solution.py:32
  26.6 11.0 %collective-permute-start.2 = (bf16[256,512]{1,0:T(8,128)(2,1)S(1)}, bf16[256,512]{1,0:T(8,128)(2,1)S(1)}, u32[]{:S(2)}, u32[]{:S(2)}) collective-permute-start(bf16[256,512]{1,0:T(8,128)(2,1)S(1)} %convert_element_type.17.own), channel_id=1, source_target_pairs={{0,64},{1,65},{4,68},{5,69},{8,72},{9,73},{12,76},{13,77},{64,2},{... | collective-permute-start | bytes 786440 | tf_op jit(solution)/shard_map/ppermute | solution.py:32
  38.0 2.5 %collective-permute-start.5 = (bf16[128,128]{1,0:T(8,128)(2,1)S(1)}, bf16[128,128]{1,0:T(8,128)(2,1)S(1)}, u32[]{:S(2)}, u32[]{:S(2)}) collective-permute-start(bf16[128,128]{1,0:T(8,128)(2,1)S(1)} %get-tuple-element.19), channel_id=1, source_target_pairs={{0,1},{1,0},{4,5},{5,4},{8,9},{9,8},{12,13},{13,12},{64,65},{65,64... | collective-permute-start | bytes 98312 | tf_op jit(solution)/shard_map/ppermute | solution.py:32
  56.0 12.2 %collective-permute-start.8 = (bf16[4,512,128]{2,1,0:T(8,128)(2,1)S(1)}, bf16[4,512,128]{2,1,0:T(8,128)(2,1)S(1)}, u32[]{:S(2)}, u32[]{:S(2)}) collective-permute-start(bf16[4,512,128]{2,1,0:T(8,128)(2,1)S(1)} %bitcast.11), channel_id=1, source_target_pairs={{0,48},{1,13},{4,52},{5,1},{8,56},{9,5},{12,60},{13,9},{64,112},{6... | collective-permute-start | bytes 1572872 | tf_op jit(solution)/shard_map/ppermute | solution.py:32
  58.6 9.6 %collective-permute-start.7 = (bf16[4,512,128]{2,1,0:T(8,128)(2,1)S(1)}, bf16[4,512,128]{2,1,0:T(8,128)(2,1)S(1)}, u32[]{:S(2)}, u32[]{:S(2)}) collective-permute-start(bf16[4,512,128]{2,1,0:T(8,128)(2,1)S(1)} %bitcast.12), channel_id=1, source_target_pairs={{0,16},{1,5},{4,20},{5,9},{8,24},{9,13},{12,28},{13,1},{64,80},{65... | collective-permute-start | bytes 1572872 | tf_op jit(solution)/shard_map/ppermute | solution.py:32
  58.6 15.2 %collective-permute-start.11 = (bf16[4,512,128]{2,1,0:T(8,128)(2,1)S(1)}, bf16[4,512,128]{2,1,0:T(8,128)(2,1)S(1)}, u32[]{:S(2)}, u32[]{:S(2)}) collective-permute-start(bf16[4,512,128]{2,1,0:T(8,128)(2,1)S(1)} %bitcast.13), channel_id=1, source_target_pairs={{0,1},{1,0},{4,5},{5,4},{8,9},{9,8},{12,13},{13,12},{64,65},{65,64... | collective-permute-start | bytes 1572872 | tf_op jit(solution)/shard_map/ppermute | solution.py:32
  68.2 9.7 %collective-permute-start.9 = (bf16[4,512,128]{2,1,0:T(8,128)(2,1)S(1)}, bf16[4,512,128]{2,1,0:T(8,128)(2,1)S(1)}, u32[]{:S(2)}, u32[]{:S(2)}) collective-permute-start(bf16[4,512,128]{2,1,0:T(8,128)(2,1)S(1)} %collective-permute-done.7.refs_1_), channel_id=1, source_target_pairs={{0,1},{1,0},{4,5},{5,4},{8,9},{9,8},{12,13},{13,12},{64,65},{65,64... | collective-permute-start | bytes 1572872 | tf_op jit(solution)/shard_map/ppermute | solution.py:32
  72.2 5.7 %collective-permute-start.10 = (bf16[4,512,128]{2,1,0:T(8,128)(2,1)S(1)}, bf16[4,512,128]{2,1,0:T(8,128)(2,1)S(1)}, u32[]{:S(2)}, u32[]{:S(2)}) collective-permute-start(bf16[4,512,128]{2,1,0:T(8,128)(2,1)S(1)} %collective-permute-done.8.refs_2_), channel_id=1, source_target_pairs={{0,1},{1,0},{4,5},{5,4},{8,9},{9,8},{12,13},{13,12},{64,65},{65,64... | collective-permute-start | bytes 1572872 | tf_op jit(solution)/shard_map/ppermute | solution.py:32
  72.2 9.8 %collective-permute-start.6 = (bf16[4,512,128]{2,1,0:T(8,128)(2,1)S(1)}, bf16[4,512,128]{2,1,0:T(8,128)(2,1)S(1)}, u32[]{:S(2)}, u32[]{:S(2)}) collective-permute-start(bf16[4,512,128]{2,1,0:T(8,128)(2,1)S(1)} %bitcast.15), channel_id=1, source_target_pairs={{0,32},{1,9},{4,36},{5,13},{8,40},{9,1},{12,44},{13,5},{64,96},{65... | collective-permute-start | bytes 1572872 | tf_op jit(solution)/shard_map/ppermute | solution.py:32
  81.0 4.4 %copy-start.1 = (s32[2048]{0:T(1024)S(1)}, s32[2048]{0:T(1024)}, u32[]{:S(2)}) copy-start(s32[2048]{0:T(1024)} %param.16) | copy-start | bytes 24580
  81.0 4.4 %copy-start.2 = (s32[512]{0:T(512)S(1)}, s32[512]{0:T(512)}, u32[]{:S(2)}) copy-start(s32[512]{0:T(512)} %param.17) | copy-start | bytes 6148
  82.1 3.3 %collective-permute-start.12 = (bf16[4,512,128]{2,1,0:T(8,128)(2,1)S(1)}, bf16[4,512,128]{2,1,0:T(8,128)(2,1)S(1)}, u32[]{:S(2)}, u32[]{:S(2)}) collective-permute-start(bf16[4,512,128]{2,1,0:T(8,128)(2,1)S(1)} %collective-permute-done.6.refs_0_), channel_id=1, source_target_pairs={{0,1},{1,0},{4,5},{5,4},{8,9},{9,8},{12,13},{13,12},{64,65},{65,64... | collective-permute-start | bytes 1572872 | tf_op jit(solution)/shard_map/ppermute | solution.py:32
where the time goes:
time: 88.4 us; the launch traced here: 88.2 us
  starting transfers between devices  31 us (35%)
  Pallas kernels  24.6 us (28%)
  waiting for transfers between devices  15.9 us (18%)
  blocking collectives  15.3 us (17%)
  local copies, waits for them, and re-layouts  1.11 us (1%)
    ppermute x13, starting transfers between devices, moved(): return lax.ppermute(value, AXES, pairs)  23.4 us
    ppermute x13, waiting for transfers between devices, moved(): return lax.ppermute(value, AXES, pairs)  15.9 us
    all_to_all x1, blocking collectives, copied(): lax.all_to_all(jnp.broadcast_to(value[None], (count, *value.shape)), AXES...  15.3 us
    pallas_call x4, Pallas kernels, product(): pl.pallas_call(functools.partial(kernel, sources), out_shape=out_shape, i...  11.8 us
    all_to_all x1, starting transfers between devices, local(): lax.all_to_all(jnp.broadcast_to(grads[None], (16, 8, 16, 128)), 'row', 0,...  7.59 us
    pallas_call x1, Pallas kernels, first(): pl.pallas_call(first_kernel, out_shape=(pltpu.VMEM((depth, 512), F32), pl...  6.36 us
    pallas_call x1, Pallas kernels, project(): pl.pallas_call(project_kernel, out_shape=(jax.ShapeDtypeStruct((768, 128)...  5.53 us
  transfers between devices with their start and end apart: 14, of which 6 were waited for; matrix products, arithmetic and copies ran while one was open for 0% of the time, Pallas kernels for 17%

commit v1 on v0

--- a/solution.py
+++ b/solution.py
@@ -17,6 +17,7 @@
 HBM = pl.BlockSpec(memory_space=pltpu.HBM)
 TILE = 512
 STEPS = (1, 3, 2)
+ALL, LOW, HIGH = range(4), range(2), range(2, 4)
 
 
 def linear(x, y, z, core):
@@ -85,23 +86,19 @@
                     w_out.at[rows, :], out_sorted.at[pl.ds(side * 32 + part * 8, 8), :], w_sem.at[side * 4 + part]
                 )
             )
-    for i in range(4):
-        start = (1 - half if i < 2 else half) * 512 + i % 2 * 256
-        rows = pl.ds(pl.multiple_of(start, 256), 256)
-        tiles.append(pltpu.make_async_copy(inputs.at[rows, :], inputs_in.at[i], sem.at[2 * i]))
-        tiles.append(pltpu.make_async_copy(grads.at[rows, :], grads_in.at[i], sem.at[2 * i + 1]))
+    for n in range(2):
+        rows = pl.ds(pl.multiple_of((half if n else 1 - half) * 512, 512), 512)
+        tiles.append(pltpu.make_async_copy(inputs.at[rows, :], inputs_in.at[n], sem.at[2 * n]))
+        tiles.append(pltpu.make_async_copy(grads.at[rows, :], grads_in.at[n], sem.at[2 * n + 1]))
     for copy in weights + tiles:
         copy.start()
     for copy in weights:
         copy.wait()
     for n in range(2):
-        outside, inside = [], []
-        for i in (2 * n, 2 * n + 1):
-            tiles[2 * i].wait()
-            inside.append(lax.dot_general(inputs_in[i], in_held[...], NT, preferred_element_type=F32))
-            tiles[2 * i + 1].wait()
-            outside.append(lax.dot_general(grads_in[i], out_sorted[...], NT, preferred_element_type=F32))
-        outside, inside = jnp.concatenate(outside, axis=0), jnp.concatenate(inside, axis=0)
+        tiles[2 * n].wait()
+        inside = lax.dot_general(inputs_in[n], in_held[...], NT, preferred_element_type=F32)
+        tiles[2 * n + 1].wait()
+        outside = lax.dot_general(grads_in[n], out_sorted[...], NT, preferred_element_type=F32)
         ends = ((384 * n, 384 * n + 256), (384 * n + 256, 384 * n + 384))
         for (first, last), value in zip(ends, packed(inside, outside[:, :32])):
             keep[first:last] = value
@@ -117,11 +114,11 @@
         in_specs=[HBM] * 4,
         out_specs=(VMEM, VMEM),
         scratch_shapes=[
-            pltpu.VMEM((4, 256, width), BF16),
-            pltpu.VMEM((4, 256, width), BF16),
+            pltpu.VMEM((2, 512, width), BF16),
+            pltpu.VMEM((2, 512, width), BF16),
             pltpu.VMEM((64, width), BF16),
             pltpu.VMEM((64, width), BF16),
-            pltpu.SemaphoreType.DMA((8,)),
+            pltpu.SemaphoreType.DMA((4,)),
             pltpu.SemaphoreType.DMA((9,)),
         ],
         cost_estimate=pl.CostEstimate(
@@ -197,16 +194,16 @@
     core, _ = core_and_half()
     row = lax.axis_index("row")
     total = None
-    for (other, step), block in zip(sources, blocks):
+    for (other, step, planes), block in zip(sources, blocks):
         owner = core ^ other
         line = (jnp.where(owner == 0, row >> 2, row & 3) - step) & 3
         stored = []
-        for plane in range(4):
+        for plane in planes:
             column = jnp.where(owner == 0, 8 * line + 2 * plane, 8 * plane + 2 * line + 1)
             stored.append(store[rows, pl.ds(pl.multiple_of(column * 128, 128), 128)])
         term = lax.dot_general(
             jnp.concatenate(stored, axis=1),
-            jnp.concatenate([block[plane] for plane in range(4)], axis=1),
+            jnp.concatenate([block[n] for n in range(len(planes))], axis=1),
             NT,
             preferred_element_type=F32,
         )
@@ -224,7 +221,7 @@
         copy.start()
     for i, copy in enumerate(copies):
         copy.wait()
-        out[i * TILE : (i + 1) * TILE, :] = partial_product([(0, 0)], held, [own], i)[1]
+        out[i * TILE : (i + 1) * TILE, :] = partial_product([(0, 0, ALL)], held, [own], i)[1]
 
 
 def first(store, own):
@@ -286,7 +283,7 @@
         out_specs=out_spec,
         scratch_shapes=scratch,
         cost_estimate=pl.CostEstimate(
-            flops=2 * depth * 512 * 512 * len(blocks), bytes_accessed=depth * 512 * 4, transcendentals=0
+            flops=2 * depth * 512 * 128 * sum(len(source[2]) for source in sources), bytes_accessed=depth * 512 * 4, transcendentals=0
         ),
         compiler_params=pltpu.CompilerParams(vmem_limit_bytes=12 << 20),
     )(store, *blocks, *extra)
@@ -319,7 +316,7 @@
     own = copied(mine.reshape(16, 8, 128), lambda x, y, z, core: (core, z if core else x))
     own = own.reshape(2, 4, 2, 16, 8, 128).transpose(1, 0, 3, 2, 4, 5).reshape(4, 512, 128)
     near = {}
-    for step in STEPS:
+    for step in (1, 3):
         near[step] = along_line(own, step)
     own_far = across(own)
     part, store = first(store_grads, own)
@@ -330,17 +327,18 @@
         return product(kernel, sources, store, blocks, before, out, VMEM, [])
 
     near[1], near[3], part = lax.optimization_barrier((near[1], near[3], part))
+    passed_1 = along_line(near[1][:2], 1)
+    passed_3 = along_line(near[3][2:], 3)
     far = dict((step, across(near[step])) for step in (1, 3))
-    part = added(next_kernel, [(1, 0), (0, 1), (0, 3)], [own_far, near[1], near[3]], [part])
-    part = added(next_kernel, [(1, 1), (1, 3)], [far[1], far[3]], [part])
-    near[2], part = lax.optimization_barrier((near[2], part))
-    far[2] = across(near[2])
-    part = added(next_kernel, [(0, 2)], [near[2]], [part])
+    part = added(next_kernel, [(1, 0, ALL), (0, 1, ALL), (0, 3, ALL)], [own_far, near[1], near[3]], [part])
+    passed_1, passed_3, part = lax.optimization_barrier((passed_1, passed_3, part))
+    far_1, far_3 = across(passed_1), across(passed_3)
+    part = added(next_kernel, [(1, 1, ALL), (1, 3, ALL)], [far[1], far[3]], [part])
     return product(
         last_kernel,
-        [(1, 2)],
+        [(0, 2, LOW), (0, 2, HIGH), (1, 2, LOW), (1, 2, HIGH)],
         store,
-        [far[2]],
+        [passed_1, passed_3, far_1, far_3],
         [part, store_order.reshape(depth // 128, 128), example_ids[None, :]],
         jax.ShapeDtypeStruct((depth, 512), BF16),
         HBM,

time: 88.4 us -> 84.3 us (0.954)
  Pallas kernels: 24.6 us -> 23.1 us
  waiting for transfers between devices: 15.9 us -> 14.6 us
  blocking collectives: 15.3 us -> 14.3 us
    ppermute x13 -> x15, waiting for transfers between devices: 15.9 us -> 14.6 us  [moved(): return lax.ppermute(value, AXES, pairs)]
    all_to_all x1, blocking collectives: 15.3 us -> 14.3 us  [copied(): lax.all_to_all(jnp.broadcast_to(value[None], (count, *value.shape)), AXES...]
    pallas_call x4 -> x3, Pallas kernels: 11.8 us -> 11 us  [product(): pl.pallas_call(functools.partial(kernel, sources), out_shape=out_shape, i...]
    ppermute x13 -> x15, starting transfers between devices: 23.4 us -> 23.1 us  [moved(): return lax.ppermute(value, AXES, pairs)]
  transfers between devices with their start and end apart: 14 -> 16, of which waited for: 6 -> 5; matrix products, arithmetic and copies ran while one was open for 0% -> 0% of each run, Pallas kernels for 17% -> 16%
where the time goes in v1:
time: 84.3 us; the launch traced here: 84.1 us
  starting transfers between devices  30.7 us (36%)
  Pallas kernels  23.1 us (27%)
  waiting for transfers between devices  14.6 us (17%)
  blocking collectives  14.3 us (17%)
  local copies, waits for them, and re-layouts  1.15 us (1%)
    ppermute x15, starting transfers between devices, moved(): return lax.ppermute(value, AXES, pairs)  23.1 us
    ppermute x15, waiting for transfers between devices, moved(): return lax.ppermute(value, AXES, pairs)  14.6 us
    all_to_all x1, blocking collectives, copied(): lax.all_to_all(jnp.broadcast_to(value[None], (count, *value.shape)), AXES...  14.3 us
    pallas_call x3, Pallas kernels, product(): pl.pallas_call(functools.partial(kernel, sources), out_shape=out_shape, i...  11 us
    all_to_all x1, starting transfers between devices, local(): lax.all_to_all(jnp.broadcast_to(grads[None], (16, 8, 16, 128)), 'row', 0,...  7.59 us
    pallas_call x1, Pallas kernels, first(): pl.pallas_call(first_kernel, out_shape=(pltpu.VMEM((depth, 512), F32), pl...  6.37 us
    pallas_call x1, Pallas kernels, project(): pl.pallas_call(project_kernel, out_shape=(jax.ShapeDtypeStruct((768, 128)...  4.83 us
  transfers between devices with their start and end apart: 16, of which 5 were waited for; matrix products, arithmetic and copies ran while one was open for 0% of the time, Pallas kernels for 16%

profile of v1, /device:TPU:1, one launch (start us, length us, event | category | flops | bytes accessed | tf_op | source)
XLA Modules:
  0.0 84.1 jit_solution(3726006885019664149)
XLA Ops:
  0.0 4.8 %project.1 = (bf16[768,128]{1,0:T(8,128)(2,1)S(1)}, f32[768,128]{1,0:T(8,128)S(1)}) custom-call(bf16[1024,1024]{1,0:T(8,128)(2,1)} %bitcast.18, bf16[1024,1024]{1,0:T(8,128)(2,1)} %bitcast.19, bf16[64,1024]{1,0:T(8,128)(2,1)} %w_out.1, bf16[64,1024]{1,0:T(8,128)(2,1)} %w_in.1), custom_call_target="tpu_custom_call" | custom-call | flops 268435456 | bytes 4194304 | tf_op jit(solution)/shard_map/project/pallas_call | solution.py:111
  4.8 1.5 %collective-permute-start = (bf16[768,128]{1,0:T(8,128)(2,1)S(1)}, bf16[768,128]{1,0:T(8,128)(2,1)S(1)}, u32[]{:S(2)}, u32[]{:S(2)}) collective-permute-start(bf16[768,128]{1,0:T(8,128)(2,1)S(1)} %get-tuple-element.18), channel_id=1, source_target_pairs={{0,1},{1,0},{4,5},{5,4},{8,9},{9,8},{12,13},{13,12},{64,65},{65,64... | collective-permute-start | bytes 589832 | tf_op jit(solution)/shard_map/ppermute | solution.py:33
  6.3 1.1 %collective-permute-done.came = bf16[768,128]{1,0:T(8,128)(2,1)S(1)} collective-permute-done((bf16[768,128]{1,0:T(8,128)(2,1)S(1)}, bf16[768,128]{1,0:T(8,128)(2,1)S(1)}, u32[]{:S(2)}, u32[]{:S(2)}) %collective-permute-start) | collective-permute-done | bytes 196640 | tf_op jit(solution)/shard_map/ppermute | solution.py:33
  7.4 3.1 %collective-permute-start.1 = (bf16[384,128]{1,0:T(8,128)(2,1)S(1)}, bf16[384,128]{1,0:T(8,128)(2,1)S(1)}, u32[]{:S(2)}, u32[]{:S(2)}) collective-permute-start(bf16[384,128]{1,0:T(8,128)(2,1)S(1)} %add_convert_fusion), channel_id=1, source_target_pairs={{0,2},{1,3},{4,6},{5,7},{8,10},{9,11},{12,14},{13,15},{64,66},{65,... | collective-permute-start | bytes 294920 | tf_op jit(solution)/shard_map/ppermute | solution.py:33
  10.5 2.6 %collective-permute-done.1.came_half = bf16[384,128]{1,0:T(8,128)(2,1)S(1)} collective-permute-done((bf16[384,128]{1,0:T(8,128)(2,1)S(1)}, bf16[384,128]{1,0:T(8,128)(2,1)S(1)}, u32[]{:S(2)}, u32[]{:S(2)}) %collective-permute-start.1) | collective-permute-done | bytes 98336 | tf_op jit(solution)/shard_map/ppermute | solution.py:33
  13.6 0.9 %broadcast_in_dim.16 = bf16[16,8,16,128]{3,1,2,0:T(8,128)(2,1)} broadcast(bf16[8,16,128]{2,0,1:T(8,128)(2,1)S(1)} %copy.11), dimensions={1,2,3} | broadcast | bytes 557056 | tf_op jit(solution)/shard_map/broadcast_in_dim | solution.py:313
  14.5 7.6 %all-to-all-start = ((bf16[16,8,16,128]{3,1,2,0:T(8,128)(2,1)}), bf16[16,8,16,128]{3,1,2,0:T(8,128)(2,1)S(1)}, u32[]{:S(2)}, u32[]{:S(2)}) async-start(bf16[16,8,16,128]{3,1,2,0:T(8,128)(2,1)} %broadcast_in_dim.16), calls=%async_computation | async-start | bytes 1048576 | tf_op jit(solution)/shard_map/all_to_all | solution.py:313
  22.1 1.4 %collective-permute-start.2 = (bf16[256,512]{1,0:T(8,128)(2,1)S(1)}, bf16[256,512]{1,0:T(8,128)(2,1)S(1)}, u32[]{:S(2)}, u32[]{:S(2)}) collective-permute-start(bf16[256,512]{1,0:T(8,128)(2,1)S(1)} %convert_element_type.17.own), channel_id=1, source_target_pairs={{0,64},{1,65},{4,68},{5,69},{8,72},{9,73},{12,76},{13,77},{64,2},{... | collective-permute-start | bytes 786440 | tf_op jit(solution)/shard_map/ppermute | solution.py:33
  23.5 1.5 %collective-permute-start.3 = (bf16[256,512]{1,0:T(8,128)(2,1)S(1)}, bf16[256,512]{1,0:T(8,128)(2,1)S(1)}, u32[]{:S(2)}, u32[]{:S(2)}) collective-permute-start(bf16[256,512]{1,0:T(8,128)(2,1)S(1)} %convert_element_type.17.own), channel_id=1, source_target_pairs={{0,66},{1,67},{4,70},{5,71},{8,74},{9,75},{12,78},{13,79},{64,0},{... | collective-permute-start | bytes 786440 | tf_op jit(solution)/shard_map/ppermute | solution.py:33
  25.0 1.6 %collective-permute-start.4 = (bf16[256,512]{1,0:T(8,128)(2,1)S(1)}, bf16[256,512]{1,0:T(8,128)(2,1)S(1)}, u32[]{:S(2)}, u32[]{:S(2)}) collective-permute-start(bf16[256,512]{1,0:T(8,128)(2,1)S(1)} %convert_element_type.17.own), channel_id=1, source_target_pairs={{0,2},{1,3},{4,6},{5,7},{8,10},{9,11},{12,14},{13,15},{64,66},{65,... | collective-permute-start | bytes 786440 | tf_op jit(solution)/shard_map/ppermute | solution.py:33
  26.6 3.3 %collective-permute-done.2.behind = bf16[256,512]{1,0:T(8,128)(2,1)S(1)} collective-permute-done((bf16[256,512]{1,0:T(8,128)(2,1)S(1)}, bf16[256,512]{1,0:T(8,128)(2,1)S(1)}, u32[]{:S(2)}, u32[]{:S(2)}) %collective-permute-start.2) | collective-permute-done | bytes 262176 | tf_op jit(solution)/shard_map/ppermute | solution.py:33
  29.9 6.7 %collective-permute-done.4.across_ring = bf16[256,512]{1,0:T(8,128)(2,1)S(1)} collective-permute-done((bf16[256,512]{1,0:T(8,128)(2,1)S(1)}, bf16[256,512]{1,0:T(8,128)(2,1)S(1)}, u32[]{:S(2)}, u32[]{:S(2)}) %collective-permute-start.4) | collective-permute-done | bytes 262176 | tf_op jit(solution)/shard_map/ppermute | solution.py:33
  37.1 2.4 %collective-permute-start.5 = (bf16[128,128]{1,0:T(8,128)(2,1)S(1)}, bf16[128,128]{1,0:T(8,128)(2,1)S(1)}, u32[]{:S(2)}, u32[]{:S(2)}) collective-permute-start(bf16[128,128]{1,0:T(8,128)(2,1)S(1)} %get-tuple-element.20), channel_id=1, source_target_pairs={{0,1},{1,0},{4,5},{5,4},{8,9},{9,8},{12,13},{13,12},{64,65},{65,64... | collective-permute-start | bytes 98312 | tf_op jit(solution)/shard_map/ppermute | solution.py:33
  39.5 0.9 %collective-permute-done.5 = bf16[128,128]{1,0:T(8,128)(2,1)S(1)} collective-permute-done((bf16[128,128]{1,0:T(8,128)(2,1)S(1)}, bf16[128,128]{1,0:T(8,128)(2,1)S(1)}, u32[]{:S(2)}, u32[]{:S(2)}) %collective-permute-start.5) | collective-permute-done | bytes 32800 | tf_op jit(solution)/shard_map/ppermute | solution.py:33
  40.5 14.3 %all_to_all.10 = bf16[16,16,8,128]{3,2,1,0:T(8,128)(2,1)S(1)} all-to-all(bf16[16,16,8,128]{3,2,1,0:T(8,128)(2,1)S(1)} %broadcast_in_dim.18), channel_id=1, replica_groups={{0,2,4,6,8,10,12,14,64,66,68,70,72,74,76,78},{1,3,17,19,33,35,49,51,65,..., dimensions={0} | all-to-all | bytes 1048576 | tf_op jit(solution)/shard_map/all_to_all | solution.py:57
  54.9 1.3 %collective-permute-start.6 = (bf16[4,512,128]{2,1,0:T(8,128)(2,1)S(1)}, bf16[4,512,128]{2,1,0:T(8,128)(2,1)S(1)}, u32[]{:S(2)}, u32[]{:S(2)}) collective-permute-start(bf16[4,512,128]{2,1,0:T(8,128)(2,1)S(1)} %bitcast.11), channel_id=1, source_target_pairs={{0,16},{1,5},{4,20},{5,9},{8,24},{9,13},{12,28},{13,1},{64,80},{65... | collective-permute-start | bytes 1572872 | tf_op jit(solution)/shard_map/ppermute | solution.py:33
  56.2 1.5 %collective-permute-start.7 = (bf16[4,512,128]{2,1,0:T(8,128)(2,1)S(1)}, bf16[4,512,128]{2,1,0:T(8,128)(2,1)S(1)}, u32[]{:S(2)}, u32[]{:S(2)}) collective-permute-start(bf16[4,512,128]{2,1,0:T(8,128)(2,1)S(1)} %bitcast.12), channel_id=1, source_target_pairs={{0,48},{1,13},{4,52},{5,1},{8,56},{9,5},{12,60},{13,9},{64,112},{6... | collective-permute-start | bytes 1572872 | tf_op jit(solution)/shard_map/ppermute | solution.py:33
  57.7 4.0 %collective-permute-start.10 = (bf16[4,512,128]{2,1,0:T(8,128)(2,1)S(1)}, bf16[4,512,128]{2,1,0:T(8,128)(2,1)S(1)}, u32[]{:S(2)}, u32[]{:S(2)}) collective-permute-start(bf16[4,512,128]{2,1,0:T(8,128)(2,1)S(1)} %bitcast.13), channel_id=1, source_target_pairs={{0,1},{1,0},{4,5},{5,4},{8,9},{9,8},{12,13},{13,12},{64,65},{65,64... | collective-permute-start | bytes 1572872 | tf_op jit(solution)/shard_map/ppermute | solution.py:33
  61.7 6.4 %first.1 = (f32[2048,512]{1,0:T(8,128)S(1)}, bf16[2048,4096]{1,0:T(8,128)(2,1)S(1)}) custom-call(bf16[2048,4096]{1,0:T(8,128)(2,1)} %store.1, bf16[4,512,128]{2,1,0:T(8,128)(2,1)S(1)} %bitcast.14), custom_call_target="tpu_custom_call" | custom-call | flops 1073741824 | bytes 33554432 | tf_op jit(solution)/shard_map/first/pallas_call | solution.py:229
  69.1 2.6 %collective-permute-start.9 = (bf16[2,512,128]{2,1,0:T(8,128)(2,1)S(1)}, bf16[2,512,128]{2,1,0:T(8,128)(2,1)S(1)}, u32[]{:S(2)}, u32[]{:S(2)}) collective-permute-start(bf16[2,512,128]{2,1,0:T(8,128)(2,1)S(1)} %slice.15), channel_id=1, source_target_pairs={{0,48},{1,13},{4,52},{5,1},{8,56},{9,5},{12,60},{13,9},{64,112},{6... | collective-permute-start | bytes 786440 | tf_op jit(solution)/shard_map/ppermute | solution.py:33
  71.7 4.1 %shard_map.91.refs_2_ = f32[2048,512]{1,0:T(8,128)S(1)} custom-call(bf16[2048,4096]{1,0:T(8,128)(2,1)S(1)} %get-tuple-element.21.store, bf16[4,512,128]{2,1,0:T(8,128)(2,1)S(1)} %collective-permute-done.10.refs_0_, bf16[4,512,128]{2,1,0:T(8,128)(2,1)S(1)} %collective-permute-done.6.refs_1_, bf16[4,512,128]{2,1,0:T(8,128)(2,1)S(1)} %collective-permute-done.7.refs_2_, ...), custom_call_target="tpu_custom_call" | custom-call | flops 3221225472 | bytes 4194304 | tf_op jit(solution)/shard_map/pallas_call | solution.py:279
  75.8 1.3 %collective-permute-start.11 = (bf16[2,512,128]{2,1,0:T(8,128)(2,1)S(1)}, bf16[2,512,128]{2,1,0:T(8,128)(2,1)S(1)}, u32[]{:S(2)}, u32[]{:S(2)}) collective-permute-start(bf16[2,512,128]{2,1,0:T(8,128)(2,1)S(1)} %collective-permute-done.8.refs_0_), channel_id=1, source_target_pairs={{0,1},{1,0},{4,5},{5,4},{8,9},{9,8},{12,13},{13,12},{64,65},{65,64... | collective-permute-start | bytes 786440 | tf_op jit(solution)/shard_map/ppermute | solution.py:33
  77.2 3.0 %shard_map.92.refs_4_ = f32[2048,512]{1,0:T(8,128)S(1)} custom-call(bf16[2048,4096]{1,0:T(8,128)(2,1)S(1)} %get-tuple-element.21.store, bf16[4,512,128]{2,1,0:T(8,128)(2,1)S(1)} %collective-permute-done.13.refs_0_, bf16[4,512,128]{2,1,0:T(8,128)(2,1)S(1)} %collective-permute-done.14.refs_1_, f32[2048,512]{1,0:T(8,128)S(1)} %shard_map.91.refs_2_), custom_call_target="tpu_custom_call" | custom-call | flops 2147483648 | bytes 4194304 | tf_op jit(solution)/shard_map/pallas_call | solution.py:279
  80.2 3.9 %shard_map.93 = bf16[2048,512]{1,0:T(8,128)(2,1)} custom-call(bf16[2048,4096]{1,0:T(8,128)(2,1)S(1)} %get-tuple-element.21.store, bf16[2,512,128]{2,1,0:T(8,128)(2,1)S(1)} %collective-permute-done.8.refs_0_, bf16[2,512,128]{2,1,0:T(8,128)(2,1)S(1)} %collective-permute-done.9.refs_1_, bf16[2,512,128]{2,1,0:T(8,128)(2,1)S(1)} %collective-permute-done.11.refs_2_, ...), custom_call_target="tpu_custom_call" | custom-call | flops 2147483648 | bytes 4194304 | tf_op jit(solution)/shard_map/pallas_call | solution.py:279
  (33 shorter events, 2.2 us)
Async XLA Ops:
  0.0 13.1 %copy-start = (s32[16,64]{1,0:T(8,128)S(1)}, s32[16,64]{1,0:T(8,128)}, u32[]{:S(2)}) copy-start(s32[16,64]{1,0:T(8,128)} %ids.1) | copy-start | bytes 12292
  0.0 22.1 %copy-start.3 = (f32[256,512]{1,0:T(8,128)S(1)}, f32[256,512]{1,0:T(8,128)}, u32[]{:S(2)}) copy-start(f32[256,512]{1,0:T(8,128)} %param.14) | copy-start | bytes 1572868
  4.8 2.5 %collective-permute-start = (bf16[768,128]{1,0:T(8,128)(2,1)S(1)}, bf16[768,128]{1,0:T(8,128)(2,1)S(1)}, u32[]{:S(2)}, u32[]{:S(2)}) collective-permute-start(bf16[768,128]{1,0:T(8,128)(2,1)S(1)} %get-tuple-element.18), channel_id=1, source_target_pairs={{0,1},{1,0},{4,5},{5,4},{8,9},{9,8},{12,13},{13,12},{64,65},{65,64... | collective-permute-start | bytes 589832 | tf_op jit(solution)/shard_map/ppermute | solution.py:33
  7.4 5.7 %collective-permute-start.1 = (bf16[384,128]{1,0:T(8,128)(2,1)S(1)}, bf16[384,128]{1,0:T(8,128)(2,1)S(1)}, u32[]{:S(2)}, u32[]{:S(2)}) collective-permute-start(bf16[384,128]{1,0:T(8,128)(2,1)S(1)} %add_convert_fusion), channel_id=1, source_target_pairs={{0,2},{1,3},{4,6},{5,7},{8,10},{9,11},{12,14},{13,15},{64,66},{65,... | collective-permute-start | bytes 294920 | tf_op jit(solution)/shard_map/ppermute | solution.py:33
  14.5 22.1 %all-to-all-start = ((bf16[16,8,16,128]{3,1,2,0:T(8,128)(2,1)}), bf16[16,8,16,128]{3,1,2,0:T(8,128)(2,1)S(1)}, u32[]{:S(2)}, u32[]{:S(2)}) async-start(bf16[16,8,16,128]{3,1,2,0:T(8,128)(2,1)} %broadcast_in_dim.16), calls=%async_computation | async-start | bytes 1048576 | tf_op jit(solution)/shard_map/all_to_all | solution.py:313
  22.1 7.8 %collective-permute-start.2 = (bf16[256,512]{1,0:T(8,128)(2,1)S(1)}, bf16[256,512]{1,0:T(8,128)(2,1)S(1)}, u32[]{:S(2)}, u32[]{:S(2)}) collective-permute-start(bf16[256,512]{1,0:T(8,128)(2,1)S(1)} %convert_element_type.17.own), channel_id=1, source_target_pairs={{0,64},{1,65},{4,68},{5,69},{8,72},{9,73},{12,76},{13,77},{64,2},{... | collective-permute-start | bytes 786440 | tf_op jit(solution)/shard_map/ppermute | solution.py:33
  23.5 6.4 %collective-permute-start.3 = (bf16[256,512]{1,0:T(8,128)(2,1)S(1)}, bf16[256,512]{1,0:T(8,128)(2,1)S(1)}, u32[]{:S(2)}, u32[]{:S(2)}) collective-permute-start(bf16[256,512]{1,0:T(8,128)(2,1)S(1)} %convert_element_type.17.own), channel_id=1, source_target_pairs={{0,66},{1,67},{4,70},{5,71},{8,74},{9,75},{12,78},{13,79},{64,0},{... | collective-permute-start | bytes 786440 | tf_op jit(solution)/shard_map/ppermute | solution.py:33
  25.0 11.6 %collective-permute-start.4 = (bf16[256,512]{1,0:T(8,128)(2,1)S(1)}, bf16[256,512]{1,0:T(8,128)(2,1)S(1)}, u32[]{:S(2)}, u32[]{:S(2)}) collective-permute-start(bf16[256,512]{1,0:T(8,128)(2,1)S(1)} %convert_element_type.17.own), channel_id=1, source_target_pairs={{0,2},{1,3},{4,6},{5,7},{8,10},{9,11},{12,14},{13,15},{64,66},{65,... | collective-permute-start | bytes 786440 | tf_op jit(solution)/shard_map/ppermute | solution.py:33
  37.1 3.3 %collective-permute-start.5 = (bf16[128,128]{1,0:T(8,128)(2,1)S(1)}, bf16[128,128]{1,0:T(8,128)(2,1)S(1)}, u32[]{:S(2)}, u32[]{:S(2)}) collective-permute-start(bf16[128,128]{1,0:T(8,128)(2,1)S(1)} %get-tuple-element.20), channel_id=1, source_target_pairs={{0,1},{1,0},{4,5},{5,4},{8,9},{9,8},{12,13},{13,12},{64,65},{65,64... | collective-permute-start | bytes 98312 | tf_op jit(solution)/shard_map/ppermute | solution.py:33
  54.9 13.2 %collective-permute-start.6 = (bf16[4,512,128]{2,1,0:T(8,128)(2,1)S(1)}, bf16[4,512,128]{2,1,0:T(8,128)(2,1)S(1)}, u32[]{:S(2)}, u32[]{:S(2)}) collective-permute-start(bf16[4,512,128]{2,1,0:T(8,128)(2,1)S(1)} %bitcast.11), channel_id=1, source_target_pairs={{0,16},{1,5},{4,20},{5,9},{8,24},{9,13},{12,28},{13,1},{64,80},{65... | collective-permute-start | bytes 1572872 | tf_op jit(solution)/shard_map/ppermute | solution.py:33
  56.2 11.9 %collective-permute-start.7 = (bf16[4,512,128]{2,1,0:T(8,128)(2,1)S(1)}, bf16[4,512,128]{2,1,0:T(8,128)(2,1)S(1)}, u32[]{:S(2)}, u32[]{:S(2)}) collective-permute-start(bf16[4,512,128]{2,1,0:T(8,128)(2,1)S(1)} %bitcast.12), channel_id=1, source_target_pairs={{0,48},{1,13},{4,52},{5,1},{8,56},{9,5},{12,60},{13,9},{64,112},{6... | collective-permute-start | bytes 1572872 | tf_op jit(solution)/shard_map/ppermute | solution.py:33
  57.7 14.0 %collective-permute-start.10 = (bf16[4,512,128]{2,1,0:T(8,128)(2,1)S(1)}, bf16[4,512,128]{2,1,0:T(8,128)(2,1)S(1)}, u32[]{:S(2)}, u32[]{:S(2)}) collective-permute-start(bf16[4,512,128]{2,1,0:T(8,128)(2,1)S(1)} %bitcast.13), channel_id=1, source_target_pairs={{0,1},{1,0},{4,5},{5,4},{8,9},{9,8},{12,13},{13,12},{64,65},{65,64... | collective-permute-start | bytes 1572872 | tf_op jit(solution)/shard_map/ppermute | solution.py:33
  68.1 9.1 %collective-permute-start.13 = (bf16[4,512,128]{2,1,0:T(8,128)(2,1)S(1)}, bf16[4,512,128]{2,1,0:T(8,128)(2,1)S(1)}, u32[]{:S(2)}, u32[]{:S(2)}) collective-permute-start(bf16[4,512,128]{2,1,0:T(8,128)(2,1)S(1)} %collective-permute-done.6.refs_1_), channel_id=1, source_target_pairs={{0,1},{1,0},{4,5},{5,4},{8,9},{9,8},{12,13},{13,12},{64,65},{65,64... | collective-permute-start | bytes 1572872 | tf_op jit(solution)/shard_map/ppermute | solution.py:33
  68.9 8.3 %collective-permute-start.14 = (bf16[4,512,128]{2,1,0:T(8,128)(2,1)S(1)}, bf16[4,512,128]{2,1,0:T(8,128)(2,1)S(1)}, u32[]{:S(2)}, u32[]{:S(2)}) collective-permute-start(bf16[4,512,128]{2,1,0:T(8,128)(2,1)S(1)} %collective-permute-done.7.refs_2_), channel_id=1, source_target_pairs={{0,1},{1,0},{4,5},{5,4},{8,9},{9,8},{12,13},{13,12},{64,65},{65,64... | collective-permute-start | bytes 1572872 | tf_op jit(solution)/shard_map/ppermute | solution.py:33
  68.9 6.9 %collective-permute-start.8 = (bf16[2,512,128]{2,1,0:T(8,128)(2,1)S(1)}, bf16[2,512,128]{2,1,0:T(8,128)(2,1)S(1)}, u32[]{:S(2)}, u32[]{:S(2)}) collective-permute-start(bf16[2,512,128]{2,1,0:T(8,128)(2,1)S(1)} %slice.14), channel_id=1, source_target_pairs={{0,16},{1,5},{4,20},{5,9},{8,24},{9,13},{12,28},{13,1},{64,80},{65... | collective-permute-start | bytes 786440 | tf_op jit(solution)/shard_map/ppermute | solution.py:33
  69.1 6.7 %collective-permute-start.9 = (bf16[2,512,128]{2,1,0:T(8,128)(2,1)S(1)}, bf16[2,512,128]{2,1,0:T(8,128)(2,1)S(1)}, u32[]{:S(2)}, u32[]{:S(2)}) collective-permute-start(bf16[2,512,128]{2,1,0:T(8,128)(2,1)S(1)} %slice.15), channel_id=1, source_target_pairs={{0,48},{1,13},{4,52},{5,1},{8,56},{9,5},{12,60},{13,9},{64,112},{6... | collective-permute-start | bytes 786440 | tf_op jit(solution)/shard_map/ppermute | solution.py:33
  75.8 4.4 %copy-start.1 = (s32[2048]{0:T(1024)S(1)}, s32[2048]{0:T(1024)}, u32[]{:S(2)}) copy-start(s32[2048]{0:T(1024)} %param.16) | copy-start | bytes 24580
  75.8 4.4 %copy-start.2 = (s32[512]{0:T(512)S(1)}, s32[512]{0:T(512)}, u32[]{:S(2)}) copy-start(s32[512]{0:T(512)} %param.17) | copy-start | bytes 6148
  75.8 4.4 %collective-permute-start.11 = (bf16[2,512,128]{2,1,0:T(8,128)(2,1)S(1)}, bf16[2,512,128]{2,1,0:T(8,128)(2,1)S(1)}, u32[]{:S(2)}, u32[]{:S(2)}) collective-permute-start(bf16[2,512,128]{2,1,0:T(8,128)(2,1)S(1)} %collective-permute-done.8.refs_0_), channel_id=1, source_target_pairs={{0,1},{1,0},{4,5},{5,4},{8,9},{9,8},{12,13},{13,12},{64,65},{65,64... | collective-permute-start | bytes 786440 | tf_op jit(solution)/shard_map/ppermute | solution.py:33
  77.2 3.1 %collective-permute-start.12 = (bf16[2,512,128]{2,1,0:T(8,128)(2,1)S(1)}, bf16[2,512,128]{2,1,0:T(8,128)(2,1)S(1)}, u32[]{:S(2)}, u32[]{:S(2)}) collective-permute-start(bf16[2,512,128]{2,1,0:T(8,128)(2,1)S(1)} %collective-permute-done.9.refs_1_), channel_id=1, source_target_pairs={{0,1},{1,0},{4,5},{5,4},{8,9},{9,8},{12,13},{13,12},{64,65},{65,64... | collective-permute-start | bytes 786440 | tf_op jit(solution)/shard_map/ppermute | solution.py:33
